TPU v7x, 32 devices: a whole 2x2x4 slice. The times are simulated.
32 devices in a mesh: ctx: 8 (over z, x), tp: 4 (over y, core).
Axes of the slice: x: 2, y: 2, z: 4, core: 2. Of those that a mesh axis runs over, the one named last changes fastest.
Arguments:
- hidden: bfloat16 [1024, 3584], P('ctx', 'tp'), may hold values from -6 to 6
- norm_gain: float32 [3584], replicated, may hold values from 0.1 to 1.9
- w_query: bfloat16 [3584, 3584], P(None, 'tp'), may hold values from -0.09375 to 0.09375
- bias_query: float32 [3584], P('tp'), may hold values from -3 to 3
- w_key: bfloat16 [3584, 512], P(None, 'tp'), may hold values from -0.09375 to 0.09375
- bias_key: float32 [512], P('tp'), may hold values from -3 to 3
- w_value: bfloat16 [3584, 512], P(None, 'tp'), may hold values from -0.09375 to 0.09375
- bias_value: float32 [512], P('tp'), may hold values from -3 to 3
- cache_key: bfloat16 [2048, 512], P('ctx', 'tp'), may hold values from -64 to 64
- cache_value: bfloat16 [2048, 512], P('ctx', 'tp'), may hold values from -6 to 6
- keep: int32 [1024], replicated, may hold values from 0 to 1, as said below
- positions: int32 [3, 1024], replicated, may hold values from 0 to 2047
Outputs:
- attended: bfloat16 [1024, 3584], P('ctx', 'tp')
Inputs may be any that keep to these rules, and one draw needn't show every extreme that they name: `keep`: exactly 512 tokens are kept; the counts kept by the 128-token blocks differ widely, and some block keeps all of its tokens.
All inputs are finite; a program needn't handle non-finite values.
Results may differ from a plain program's by a relative error of at most 0.0075.
The roundings to bfloat16 on the way count: a program that leaves them out, or rounds other values in their place, can miss the bound.
Values may be sent and summed in bfloat16 or wider, within the bound.
No kernel may reach another device: no remote copies, remote signals or barrier semaphores. Data moves between devices by JAX's collectives and lax.ppermute only.
A program may use at most 128 MiB of HBM per device.

v0:
```python
import jax
import jax.numpy as jnp
from jax import lax
from jax.sharding import PartitionSpec as P

HD = 128


def rotate(flat, where):
    count = flat.shape[0]
    heads = flat.shape[1] // HD
    x = flat.reshape(count, heads, HD)
    half = HD // 2
    freq = jnp.arange(half)
    inv = jnp.exp(-(2.0 * freq.astype(jnp.float32) / HD) * jnp.log(jnp.float32(1000000.0)))
    section = jnp.where(freq < HD // 8, 0, jnp.where(freq < HD // 8 + 3 * HD // 16, 1, 2))
    picked = where[section, :].astype(jnp.float32).T
    angle = picked * inv[None, :]
    cosine = jnp.concatenate([jnp.cos(angle), jnp.cos(angle)], axis=1)[:, None, :]
    sine = jnp.concatenate([jnp.sin(angle), jnp.sin(angle)], axis=1)[:, None, :]
    turned = jnp.concatenate([-x[:, :, half:], x[:, :, :half]], axis=2)
    return (x * cosine + turned * sine).reshape(count, heads * HD)


def local(
    hidden,
    norm_gain,
    w_query,
    bias_query,
    w_key,
    bias_key,
    w_value,
    bias_value,
    cache_key,
    cache_value,
    keep,
    positions,
):
    n_ctx = lax.axis_size("ctx")
    rank = lax.axis_index("ctx")
    tok_rows = hidden.shape[0]
    cache_rows = cache_key.shape[0]
    kv_local = w_key.shape[1] // HD
    groups = w_query.shape[1] // w_key.shape[1]
    keep_blocks = keep.reshape(n_ctx, tok_rows)
    counts = jnp.sum(keep_blocks, axis=1)
    first = jnp.cumsum(counts) - counts
    ordinal_blocks = jnp.cumsum(keep_blocks, axis=1) - keep_blocks + first[:, None]
    own_start = rank * tok_rows
    own_keep = lax.dynamic_index_in_dim(keep_blocks, rank, 0, keepdims=False)
    own_order = lax.dynamic_index_in_dim(ordinal_blocks, rank, 0, keepdims=False)
    sentinel = 2**30
    query_live = own_keep.astype(jnp.float32)
    where = lax.dynamic_slice_in_dim(positions, own_start, tok_rows, 1)
    fresh_tag = jnp.where(keep_blocks > 0, ordinal_blocks, sentinel)
    count_rows = hidden.shape[0]
    key_tag = jnp.concatenate(
        [jnp.full((n_ctx, cache_rows), -1, jnp.int32), fresh_tag], axis=1
    ).reshape(-1)
    whole = lax.all_gather(hidden, "tp", axis=1, tiled=True)
    widened = whole.astype(jnp.float32)
    scale_row = lax.rsqrt(jnp.mean(widened * widened, axis=1, keepdims=True) + 1e-06)
    normed = (widened * scale_row * norm_gain[None, :]).astype(jnp.bfloat16)
    query = rotate(
        jnp.dot(normed, w_query, preferred_element_type=jnp.float32) + bias_query, where
    ).astype(jnp.bfloat16)
    query = query.reshape(count_rows, kv_local, groups, HD)
    fresh_key = rotate(
        jnp.dot(normed, w_key, preferred_element_type=jnp.float32) + bias_key, where
    ).astype(jnp.bfloat16)
    fresh_value = (
        jnp.dot(normed, w_value, preferred_element_type=jnp.float32) + bias_value
    ).astype(jnp.bfloat16)
    keys = jnp.concatenate([cache_key, fresh_key], axis=0)
    values = jnp.concatenate([cache_value, fresh_value], axis=0)
    block_rows = cache_rows + count_rows
    factor = 1.0 / jnp.sqrt(jnp.float32(HD))

    def absorb(carry, key_piece, value_piece, start):
        peak, total, summed = carry
        count = key_piece.shape[0]
        tag = lax.dynamic_slice_in_dim(key_tag, start, count)
        seen = tag[None, :] <= own_order[:, None]
        score = (
            jnp.einsum(
                "qhgd,khd->hgqk",
                query,
                key_piece.reshape(count, kv_local, HD),
                preferred_element_type=jnp.float32,
            )
            * factor
        )
        score = jnp.where(seen[None, None], score, -jnp.inf)
        higher = jnp.maximum(peak, jnp.max(score, axis=-1))
        shrink = jnp.exp(peak - higher)
        weights = jnp.exp(score - higher[..., None])
        total = total * shrink + jnp.sum(weights, axis=-1)
        added = jnp.einsum(
            "hgqk,khd->hgqd",
            weights.astype(jnp.bfloat16),
            value_piece.reshape(count, kv_local, HD),
            preferred_element_type=jnp.float32,
        )
        summed = summed * shrink[..., None] + added
        return (higher, total, summed)

    initial = (
        jnp.full((kv_local, groups, count_rows), -1e30, jnp.float32),
        jnp.zeros((kv_local, groups, count_rows), jnp.float32),
        jnp.zeros((kv_local, groups, count_rows, HD), jnp.float32),
    )
    carry = initial
    key_piece = lax.all_gather(keys, "ctx", axis=0, tiled=True)
    value_piece = lax.all_gather(values, "ctx", axis=0, tiled=True)
    count = key_piece.shape[0]
    number = count // block_rows
    key_blocks = key_piece.reshape(number, block_rows, key_piece.shape[1])
    value_blocks = value_piece.reshape(number, block_rows, value_piece.shape[1])
    starts = jnp.arange(number) * block_rows

    def advance(state, item):
        return (absorb(state, item[0], item[1], item[2]), None)

    carry, unused = lax.scan(advance, carry, (key_blocks, value_blocks, starts))
    peak, total, summed = carry
    result = summed / total[..., None]
    result = jnp.transpose(result, (2, 0, 1, 3)).reshape(count_rows, kv_local * groups * HD)
    result = (result * query_live[:, None]).astype(jnp.bfloat16)
    return result


def solution(mesh):
    in_specs = (
        P("ctx", "tp"),
        P(),
        P(None, "tp"),
        P("tp"),
        P(None, "tp"),
        P("tp"),
        P(None, "tp"),
        P("tp"),
        P("ctx", "tp"),
        P("ctx", "tp"),
        P(),
        P(),
    )
    out_specs = P("ctx", "tp")
    return jax.shard_map(local, mesh=mesh, in_specs=in_specs, out_specs=out_specs, check_vma=False)
```

profile of v0, /device:TPU:0, one launch (start us, length us, event | category | flops | bytes accessed | tf_op | source)
XLA Modules:
  0.0 137.8 jit_solution(11754912918624157827)
XLA Ops:
  0.0 0.8 constant_dynamic-slice_fusion.1
  0.8 0.6 gather_fusion
  1.4 0.2 cosine_bitcast_fusion
  1.6 11.0 %all_gather.9 = bf16[128,3584]{1,0:T(8,128)(2,1)S(1)} all-gather(bf16[128,896]{1,0:T(8,128)(2,1)} %param.14), channel_id=1, replica_groups=mesh['ctx'=8,'tp'=4] {'tp'}, dimensions={1}, use_global_device_ids=true | all-gather | bytes 1146880 | tf_op jit(solution)/shard_map/all_gather | solution.py:60
  12.6 0.3 fusion.18
  12.9 0.6 convolution_add_fusion.2
  13.6 4.0 %convolution_add_fusion = f32[128,896]{1,0:T(8,128)S(1)} fusion(bf16[3584,896]{1,0:T(8,128)(2,1)} %param.16, f32[896]{0:T(1024)S(1)} %copy-done.6, bf16[128,3584]{1,0:T(8,128)(2,1)S(1)} %all_gather.9, f32[3584]{0:T(1024)S(1)} %copy-done.4, f32[128]{0:T(128)S(1)} %add_rsqrt_fusion), kind=kOutput, calls=%fused_computation.33 | convolution fusion | flops 824033280 | bytes 7817216 | tf_op jit(solution)/shard_map/dot_general | solution.py:65
  17.6 0.2 copy.22
  17.9 0.2 copy.23
  18.1 0.8 mul.122
  18.9 1.2 copy.21
  20.3 0.2 copy.24
  20.5 0.2 copy.25
  20.7 0.1 copy.20
  20.8 34.0 %all_gather.10 = bf16[3072,128]{1,0:T(8,128)(2,1)} all-gather(bf16[384,128]{1,0:T(8,128)(2,1)S(1)} %pad_maximum_fusion), channel_id=1, replica_groups=mesh['ctx'=8,'tp'=4] {'ctx'}, dimensions={0}, use_global_device_ids=true | all-gather | bytes 884736 | tf_op jit(solution)/shard_map/all_gather | solution.py:113
  54.8 0.1 bitcast_reduce_fusion
  54.9 0.2 reduce-window.8
  55.1 0.3 reduce_window_sum.18
  55.5 0.5 fusion.21
  56.0 34.0 %all_gather.11 = bf16[3072,128]{1,0:T(8,128)(2,1)} all-gather(bf16[384,128]{1,0:T(8,128)(2,1)S(1)} %pad_maximum_fusion.1), channel_id=1, replica_groups=mesh['ctx'=8,'tp'=4] {'ctx'}, dimensions={0}, use_global_device_ids=true | all-gather | bytes 884736 | tf_op jit(solution)/shard_map/all_gather | solution.py:114
  90.0 46.6 %while.15 = (s32[]{:T(128)}, f32[1,7,128]{2,1,0:T(8,128)S(1)}, f32[1,7,128]{2,1,0:T(8,128)S(1)}, f32[1,7,128,128]{3,2,1,0:T(8,128)S(1)}, s32[8]{0:T(128)S(1)}, /...) while((s32[]{:T(128)}, f32[1,7,128]{2,1,0:T(8,128)S(1)}, ...), condition=%wide.region_7.8_spmd.clone, body=%wide.region_4.7_spmd.clone.sunk | while | flops 179655936 | bytes 5732539 | solution.py:124
  90.0 0.7 dynamic_slice.56
  92.7 0.1 broadcast_compare_fusion.2
  92.8 1.3 select_reduce_fusion.2
  94.1 1.4 %fusion.45 = f32[1,7,128,128]{3,2,1,0:T(8,128)S(1)} fusion(f32[1,7,128,384]{2,3,1,0:T(8,128)S(1)} %get-tuple-element.215, f32[7,128]{1,0:T(8,128)S(1)} %bitcast.92, pred[128,384]{0,1:T(8,128)(4,1)S(1)} %broadcast_compare_fusion.2, f32[1,7,128,128]{3,2,1,0:T(8,128)S(1)} %get-tuple-element.233, f32[7,128]{1,0:T(8,128)S(1)} %get-tuple-element.216, ...), kind=kOutput, calls=%fused_computation.6.clone.1 | convolution fusion | flops 89456640 | bytes 2448897 | tf_op jit(solution)/shard_map/while/body/eval_jaxpr/hgqk,khd->hgqd/dot_general | solution.py:98
  95.6 0.3 fusion.44
  95.9 0.7 dynamic_slice.56
  98.4 0.1 dynamic_slice.57
  98.5 0.1 broadcast_compare_fusion.2
  98.7 1.3 select_reduce_fusion.2
  100.0 1.4 %fusion.45 = f32[1,7,128,128]{3,2,1,0:T(8,128)S(1)} fusion(f32[1,7,128,384]{2,3,1,0:T(8,128)S(1)} %get-tuple-element.215, f32[7,128]{1,0:T(8,128)S(1)} %bitcast.92, pred[128,384]{0,1:T(8,128)(4,1)S(1)} %broadcast_compare_fusion.2, f32[1,7,128,128]{3,2,1,0:T(8,128)S(1)} %get-tuple-element.233, f32[7,128]{1,0:T(8,128)S(1)} %get-tuple-element.216, ...), kind=kOutput, calls=%fused_computation.6.clone.1 | convolution fusion | flops 89456640 | bytes 2448897 | tf_op jit(solution)/shard_map/while/body/eval_jaxpr/hgqk,khd->hgqd/dot_general | solution.py:98
  101.4 0.3 fusion.44
  101.7 0.7 dynamic_slice.56
  104.4 0.1 broadcast_compare_fusion.2
  104.5 1.3 select_reduce_fusion.2
  105.8 1.4 %fusion.45 = f32[1,7,128,128]{3,2,1,0:T(8,128)S(1)} fusion(f32[1,7,128,384]{2,3,1,0:T(8,128)S(1)} %get-tuple-element.215, f32[7,128]{1,0:T(8,128)S(1)} %bitcast.92, pred[128,384]{0,1:T(8,128)(4,1)S(1)} %broadcast_compare_fusion.2, f32[1,7,128,128]{3,2,1,0:T(8,128)S(1)} %get-tuple-element.233, f32[7,128]{1,0:T(8,128)S(1)} %get-tuple-element.216, ...), kind=kOutput, calls=%fused_computation.6.clone.1 | convolution fusion | flops 89456640 | bytes 2448897 | tf_op jit(solution)/shard_map/while/body/eval_jaxpr/hgqk,khd->hgqd/dot_general | solution.py:98
  107.2 0.3 fusion.44
  107.5 0.7 dynamic_slice.56
  110.2 0.1 broadcast_compare_fusion.2
  110.3 1.3 select_reduce_fusion.2
  111.6 1.4 %fusion.45 = f32[1,7,128,128]{3,2,1,0:T(8,128)S(1)} fusion(f32[1,7,128,384]{2,3,1,0:T(8,128)S(1)} %get-tuple-element.215, f32[7,128]{1,0:T(8,128)S(1)} %bitcast.92, pred[128,384]{0,1:T(8,128)(4,1)S(1)} %broadcast_compare_fusion.2, f32[1,7,128,128]{3,2,1,0:T(8,128)S(1)} %get-tuple-element.233, f32[7,128]{1,0:T(8,128)S(1)} %get-tuple-element.216, ...), kind=kOutput, calls=%fused_computation.6.clone.1 | convolution fusion | flops 89456640 | bytes 2448897 | tf_op jit(solution)/shard_map/while/body/eval_jaxpr/hgqk,khd->hgqd/dot_general | solution.py:98
  113.1 0.3 fusion.44
  113.4 0.7 dynamic_slice.56
  116.0 0.1 broadcast_compare_fusion.2
  116.1 1.3 select_reduce_fusion.2
  117.4 1.4 %fusion.45 = f32[1,7,128,128]{3,2,1,0:T(8,128)S(1)} fusion(f32[1,7,128,384]{2,3,1,0:T(8,128)S(1)} %get-tuple-element.215, f32[7,128]{1,0:T(8,128)S(1)} %bitcast.92, pred[128,384]{0,1:T(8,128)(4,1)S(1)} %broadcast_compare_fusion.2, f32[1,7,128,128]{3,2,1,0:T(8,128)S(1)} %get-tuple-element.233, f32[7,128]{1,0:T(8,128)S(1)} %get-tuple-element.216, ...), kind=kOutput, calls=%fused_computation.6.clone.1 | convolution fusion | flops 89456640 | bytes 2448897 | tf_op jit(solution)/shard_map/while/body/eval_jaxpr/hgqk,khd->hgqd/dot_general | solution.py:98
  118.9 0.3 fusion.44
  119.2 0.7 dynamic_slice.56
  121.8 0.1 broadcast_compare_fusion.2
  122.0 1.3 select_reduce_fusion.2
  123.3 1.4 %fusion.45 = f32[1,7,128,128]{3,2,1,0:T(8,128)S(1)} fusion(f32[1,7,128,384]{2,3,1,0:T(8,128)S(1)} %get-tuple-element.215, f32[7,128]{1,0:T(8,128)S(1)} %bitcast.92, pred[128,384]{0,1:T(8,128)(4,1)S(1)} %broadcast_compare_fusion.2, f32[1,7,128,128]{3,2,1,0:T(8,128)S(1)} %get-tuple-element.233, f32[7,128]{1,0:T(8,128)S(1)} %get-tuple-element.216, ...), kind=kOutput, calls=%fused_computation.6.clone.1 | convolution fusion | flops 89456640 | bytes 2448897 | tf_op jit(solution)/shard_map/while/body/eval_jaxpr/hgqk,khd->hgqd/dot_general | solution.py:98
  124.7 0.3 fusion.44
  125.0 0.7 dynamic_slice.56
  127.7 0.1 broadcast_compare_fusion.2
  127.8 1.3 select_reduce_fusion.2
  129.1 1.4 %fusion.45 = f32[1,7,128,128]{3,2,1,0:T(8,128)S(1)} fusion(f32[1,7,128,384]{2,3,1,0:T(8,128)S(1)} %get-tuple-element.215, f32[7,128]{1,0:T(8,128)S(1)} %bitcast.92, pred[128,384]{0,1:T(8,128)(4,1)S(1)} %broadcast_compare_fusion.2, f32[1,7,128,128]{3,2,1,0:T(8,128)S(1)} %get-tuple-element.233, f32[7,128]{1,0:T(8,128)S(1)} %get-tuple-element.216, ...), kind=kOutput, calls=%fused_computation.6.clone.1 | convolution fusion | flops 89456640 | bytes 2448897 | tf_op jit(solution)/shard_map/while/body/eval_jaxpr/hgqk,khd->hgqd/dot_general | solution.py:98
  130.5 0.3 fusion.44
  130.8 0.7 dynamic_slice.56
  133.5 0.1 broadcast_compare_fusion.2
  133.6 1.3 select_reduce_fusion.2
  134.9 1.4 %fusion.45 = f32[1,7,128,128]{3,2,1,0:T(8,128)S(1)} fusion(f32[1,7,128,384]{2,3,1,0:T(8,128)S(1)} %get-tuple-element.215, f32[7,128]{1,0:T(8,128)S(1)} %bitcast.92, pred[128,384]{0,1:T(8,128)(4,1)S(1)} %broadcast_compare_fusion.2, f32[1,7,128,128]{3,2,1,0:T(8,128)S(1)} %get-tuple-element.233, f32[7,128]{1,0:T(8,128)S(1)} %get-tuple-element.216, ...), kind=kOutput, calls=%fused_computation.6.clone.1 | convolution fusion | flops 89456640 | bytes 2448897 | tf_op jit(solution)/shard_map/while/body/eval_jaxpr/hgqk,khd->hgqd/dot_general | solution.py:98
  136.4 0.3 fusion.44
  136.7 0.2 copy.26
  137.0 0.8 copy.27
  (74 shorter events, 1.2 us)
Async XLA Ops:
  0.0 12.9 %copy-start = (bf16[3584,128]{1,0:T(8,128)(2,1)S(1)}, bf16[3584,128]{1,0:T(8,128)(2,1)}, u32[]{:S(2)}) copy-start(bf16[3584,128]{1,0:T(8,128)(2,1)} %param.18) | copy-start | bytes 2752516
  0.0 12.9 %copy-start.4 = (f32[3584]{0:T(1024)S(1)}, f32[3584]{0:T(1024)}, u32[]{:S(2)}) copy-start(f32[3584]{0:T(1024)} %param.15) | copy-start | bytes 43012
  0.0 12.9 %copy-start.8 = (f32[128]{0:T(128)S(1)}, f32[128]{0:T(128)}, u32[]{:S(2)}) copy-start(f32[128]{0:T(128)} %param.19) | copy-start | bytes 1540
  12.6 1.0 copy-start.6
  18.9 1.9 %copy-start.1 = (bf16[256,128]{1,0:T(8,128)(2,1)S(1)}, bf16[256,128]{1,0:T(8,128)(2,1)}, u32[]{:S(2)}) copy-start(bf16[256,128]{1,0:T(8,128)(2,1)} %param.22) | copy-start | bytes 196612
  20.2 34.7 %copy-start.3 = (s32[1024]{0:T(1024)S(1)}, s32[1024]{0:T(1024)}, u32[]{:S(2)}) copy-start(s32[1024]{0:T(1024)} %param.24) | copy-start | bytes 12292
  20.2 35.3 %copy-start.9 = (f32[128]{0:T(128)S(1)}, f32[128]{0:T(128)}, u32[]{:S(2)}) copy-start(f32[128]{0:T(128)} %param.21) | copy-start | bytes 1540
  20.3 35.2 %copy-start.5 = (f32[3584]{0:T(1024)S(1)}, f32[3584]{0:T(1024)}, u32[]{:S(2)}) copy-start(f32[3584]{0:T(1024)} %param.15) | copy-start | bytes 43012
  20.3 35.2 %copy-start.7 = (bf16[3584,128]{1,0:T(8,128)(2,1)S(1)}, bf16[3584,128]{1,0:T(8,128)(2,1)}, u32[]{:S(2)}) copy-start(bf16[3584,128]{1,0:T(8,128)(2,1)} %param.20) | copy-start | bytes 2752516
  20.6 35.4 %copy-start.2 = (bf16[256,128]{1,0:T(8,128)(2,1)S(1)}, bf16[256,128]{1,0:T(8,128)(2,1)}, u32[]{:S(2)}) copy-start(bf16[256,128]{1,0:T(8,128)(2,1)} %param.23) | copy-start | bytes 196612
where the time goes:
time: 139 us; the launch traced here: 138 us
  blocking collectives  79 us (57%)
  matrix products  26.8 us (19%)
  loops' own time  15.9 us (11%)
  local copies, waits for them, and re-layouts  11.2 us (8%)
  other arithmetic  4.59 us (3%)
    all_gather x1, blocking collectives, local(): key_piece = lax.all_gather(keys, 'ctx', axis=0, tiled=True)  34 us
    all_gather x1, blocking collectives, local(): value_piece = lax.all_gather(values, 'ctx', axis=0, tiled=True)  34 us
    another operation x1, loops' own time, local(): carry, unused = lax.scan(advance, carry, (key_blocks, value_blocks, starts))  15.9 us
    dot_general x8, matrix products, absorb(): jnp.einsum('hgqk,khd->hgqd', weights.astype(jnp.bfloat16), value_piece.re...  11.5 us
    all_gather x1, blocking collectives, local(): whole = lax.all_gather(hidden, 'tp', axis=1, tiled=True)  11 us
    dot_general x8, matrix products, absorb(): jnp.einsum('qhgd,khd->hgqk', query, key_piece.reshape(count, kv_local, HD...  10.2 us
    dynamic_slice x8, local copies, waits for them, and re-layouts, local(): carry, unused = lax.scan(advance, carry, (key_blocks, value_blocks, starts))  5.24 us
    dot_general x1, matrix products, local(): jnp.dot(normed, w_query, preferred_element_type=jnp.float32) + bias_query  4.02 us

commit v1 on v0

--- a/solution.py
+++ b/solution.py
@@ -36,6 +36,12 @@
     keep,
     positions,
 ):
+
+    def arrange_patch(z_in, raw):
+        piece_now = jnp.concatenate([z_in, raw], axis=1)
+        e_next = lax.all_gather(piece_now, axis_name="ctx", axis=0, tiled=True)
+        return jnp.split(e_next, [z_in.shape[1]], axis=1)
+
     n_ctx = lax.axis_size("ctx")
     rank = lax.axis_index("ctx")
     tok_rows = hidden.shape[0]
@@ -110,8 +116,7 @@
         jnp.zeros((kv_local, groups, count_rows, HD), jnp.float32),
     )
     carry = initial
-    key_piece = lax.all_gather(keys, "ctx", axis=0, tiled=True)
-    value_piece = lax.all_gather(values, "ctx", axis=0, tiled=True)
+    key_piece, value_piece = arrange_patch(keys, values)
     count = key_piece.shape[0]
     number = count // block_rows
     key_blocks = key_piece.reshape(number, block_rows, key_piece.shape[1])

time: 139 us -> 126 us (0.906)
  blocking collectives: 79 us -> 11.2 us
  waiting for transfers between devices: 0 us -> 39.2 us
  between operations: 0.27 us -> 13.7 us
    all_gather x2 -> x0, blocking collectives: 68 us -> none  [the longest x1 34 us: local(): key_piece = lax.all_gather(keys, 'ctx', axis=0, tiled=True)]
    all_gather x0 -> x1, waiting for transfers between devices: none -> 39.2 us  [arrange_patch(): e_next = lax.all_gather(piece_now, axis_name='ctx', axis=0, tiled=True)]
    split x0 -> x1, local copies, waits for them, and re-layouts: none -> 2.63 us  [arrange_patch(): return jnp.split(e_next, [z_in.shape[1]], axis=1)]
    mul x3, local copies, waits for them, and re-layouts: 2.24 us -> 0.43 us  [rotate(): return (x * cosine + turned * sine).reshape(count, heads * HD)]
  transfers between devices with their start and end apart: 0 -> 1, of which waited for: 0 -> 1; matrix products, arithmetic and copies ran while one was open for 0% -> 5% of each run, Pallas kernels for 0% -> 0%
where the time goes in v1:
time: 126 us; the launch traced here: 125 us
  waiting for transfers between devices  39.2 us (31%)
  matrix products  27.9 us (22%)
  loops' own time  16.1 us (13%)
  between operations  13.7 us (11%)
  local copies, waits for them, and re-layouts  11.5 us (9%)
  blocking collectives  11.2 us (9%)
  other arithmetic  5.23 us (4%)
    all_gather x1, waiting for transfers between devices, arrange_patch(): e_next = lax.all_gather(piece_now, axis_name='ctx', axis=0, tiled=True)  39.2 us
    another operation x1, loops' own time, local(): carry, unused = lax.scan(advance, carry, (key_blocks, value_blocks, starts))  16.1 us
    dot_general x8, matrix products, absorb(): jnp.einsum('hgqk,khd->hgqd', weights.astype(jnp.bfloat16), value_piece.re...  11.5 us
    all_gather x1, blocking collectives, local(): whole = lax.all_gather(hidden, 'tp', axis=1, tiled=True)  11.2 us
    dot_general x8, matrix products, absorb(): jnp.einsum('qhgd,khd->hgqk', query, key_piece.reshape(count, kv_local, HD...  10.2 us
    dynamic_slice x8, local copies, waits for them, and re-layouts, local(): carry, unused = lax.scan(advance, carry, (key_blocks, value_blocks, starts))  4.69 us
    dot_general x1, matrix products, local(): jnp.dot(normed, w_query, preferred_element_type=jnp.float32) + bias_query  4 us
    split x1, local copies, waits for them, and re-layouts, arrange_patch(): return jnp.split(e_next, [z_in.shape[1]], axis=1)  2.63 us
  transfers between devices with their start and end apart: 1, of which 1 were waited for; matrix products, arithmetic and copies ran while one was open for 5% of the time, Pallas kernels for 0%

profile of v1, /device:TPU:0, one launch (start us, length us, event | category | flops | bytes accessed | tf_op | source)
XLA Modules:
  0.0 124.7 jit_solution(14282304787539537300)
XLA Ops:
  6.6 11.2 %all_gather.6 = bf16[128,3584]{1,0:T(8,128)(2,1)S(1)} all-gather(bf16[128,896]{1,0:T(8,128)(2,1)} %param.14), channel_id=1, replica_groups=mesh['ctx'=8,'tp'=4] {'tp'}, dimensions={1}, use_global_device_ids=true | all-gather | bytes 1146880 | tf_op jit(solution)/shard_map/all_gather | solution.py:66
  17.8 0.3 fusion.18
  18.1 0.6 convolution_add_fusion.2
  18.7 0.7 constant_dynamic-slice_fusion.1
  19.4 0.6 gather_fusion
  20.0 0.2 cosine_bitcast_fusion
  20.2 0.1 copy.20
  20.4 1.6 %fusion.21 = bf16[128,128]{1,0:T(8,128)(2,1)S(1)} fusion(bf16[3584,128]{1,0:T(8,128)(2,1)} %param.20, f32[128]{0:T(128)S(1)} %copy-done.7, bf16[128,3584]{1,0:T(8,128)(2,1)S(1)} %all_gather.6, f32[3584]{0:T(1024)S(1)} %copy-done.4, f32[128]{0:T(128)S(1)} %add_rsqrt_fusion), kind=kOutput, calls=%fused_computation.36 | convolution fusion | flops 119308288 | bytes 1883136 | tf_op jit(solution)/shard_map/dot_general | solution.py:78
  22.0 0.7 maximum_maximum_fusion
  22.8 4.0 %convolution_add_fusion = f32[128,896]{1,0:T(8,128)S(1)} fusion(bf16[3584,896]{1,0:T(8,128)(2,1)} %param.16, f32[896]{0:T(1024)S(1)} %copy-done.5, bf16[128,3584]{1,0:T(8,128)(2,1)S(1)} %all_gather.6, f32[3584]{0:T(1024)S(1)} %copy-done.4, f32[128]{0:T(128)S(1)} %add_rsqrt_fusion), kind=kOutput, calls=%fused_computation.33 | convolution fusion | flops 824033280 | bytes 7817216 | tf_op jit(solution)/shard_map/dot_general | solution.py:71
  26.8 0.2 copy.22
  27.1 0.2 copy.23
  27.3 0.2 copy.21
  27.6 0.2 copy.24
  27.8 0.2 copy.25
  28.0 0.1 bitcast_reduce_fusion
  28.1 0.2 reduce-window.8
  28.3 0.3 reduce_window_sum.18
  28.7 39.2 %all-gather.2.cloned.1.call-done = bf16[3072,256]{1,0:T(8,128)(2,1)} async-done(((bf16[384,256]{1,0:T(8,128)(2,1)}), bf16[3072,256]{1,0:T(8,128)(2,1)}) %all-gather.2.cloned.1.call-update) | async-done | bytes 1572880 | tf_op jit(solution)/shard_map/all_gather | solution.py:42
  67.9 2.6 %fusion.33 = (bf16[3072,128]{1,0:T(8,128)(2,1)}, bf16[3072,128]{1,0:T(8,128)(2,1)}) fusion(bf16[3072,256]{1,0:T(8,128)(2,1)} %all-gather.2.cloned.1.call-done), kind=kLoop, calls=%fused_computation.72 | loop fusion | bytes 3145728 | tf_op jit(solution)/shard_map/split | solution.py:43
  70.5 46.2 %while.15 = (s32[]{:T(128)}, f32[1,7,128]{2,1,0:T(8,128)S(1)}, f32[1,7,128]{2,1,0:T(8,128)S(1)}, f32[1,7,128,128]{3,2,1,0:T(8,128)S(1)}, s32[8]{0:T(128)S(1)}, /...) while((s32[]{:T(128)}, f32[1,7,128]{2,1,0:T(8,128)S(1)}, ...), condition=%wide.region_7.8_spmd.clone, body=%wide.region_4.7_spmd.clone.sunk | while | flops 179655936 | bytes 5732539 | solution.py:129
  70.5 0.6 dynamic_slice.56
  73.1 0.1 dynamic_slice.57
  73.1 0.1 broadcast_compare_fusion.2
  73.3 1.3 %select_reduce_fusion.2 = (f32[7,128]{1,0:T(8,128)S(1)}, f32[1,7,128,384]{2,3,1,0:T(8,128)S(1)}) fusion(pred[128,384]{0,1:T(8,128)(4,1)S(1)} %broadcast_compare_fusion.2, bf16[128,1,7,128]{3,0,2,1:T(8,128)(2,1)S(1)} %get-tuple-element.255, bf16[8,384,128]{2,1,0:T(8,128)(2,1)} %get-tuple-element.254, s32[]{:T(128)} %get-tuple-element.234), kind=kOutput, calls=%fused_computation.4.clone.1 | convolution fusion | flops 89111680 | bytes 1757184 | tf_op jit(solution)/shard_map/while/body/eval_jaxpr/qhgd,khd->hgqk/dot_general | solution.py:91
  74.6 1.4 %fusion.46 = f32[1,7,128,128]{3,2,1,0:T(8,128)S(1)} fusion(f32[1,7,128,384]{2,3,1,0:T(8,128)S(1)} %get-tuple-element.219, f32[7,128]{1,0:T(8,128)S(1)} %bitcast.92, pred[128,384]{0,1:T(8,128)(4,1)S(1)} %broadcast_compare_fusion.2, f32[1,7,128,128]{3,2,1,0:T(8,128)S(1)} %get-tuple-element.237, f32[7,128]{1,0:T(8,128)S(1)} %get-tuple-element.220, ...), kind=kOutput, calls=%fused_computation.6.clone.1 | convolution fusion | flops 89456640 | bytes 2448897 | tf_op jit(solution)/shard_map/while/body/eval_jaxpr/hgqk,khd->hgqd/dot_general | solution.py:104
  76.0 0.3 fusion.45
  76.3 0.6 dynamic_slice.56
  78.9 0.1 broadcast_compare_fusion.2
  79.0 1.3 %select_reduce_fusion.2 = (f32[7,128]{1,0:T(8,128)S(1)}, f32[1,7,128,384]{2,3,1,0:T(8,128)S(1)}) fusion(pred[128,384]{0,1:T(8,128)(4,1)S(1)} %broadcast_compare_fusion.2, bf16[128,1,7,128]{3,0,2,1:T(8,128)(2,1)S(1)} %get-tuple-element.255, bf16[8,384,128]{2,1,0:T(8,128)(2,1)} %get-tuple-element.254, s32[]{:T(128)} %get-tuple-element.234), kind=kOutput, calls=%fused_computation.4.clone.1 | convolution fusion | flops 89111680 | bytes 1757184 | tf_op jit(solution)/shard_map/while/body/eval_jaxpr/qhgd,khd->hgqk/dot_general | solution.py:91
  80.3 1.4 %fusion.46 = f32[1,7,128,128]{3,2,1,0:T(8,128)S(1)} fusion(f32[1,7,128,384]{2,3,1,0:T(8,128)S(1)} %get-tuple-element.219, f32[7,128]{1,0:T(8,128)S(1)} %bitcast.92, pred[128,384]{0,1:T(8,128)(4,1)S(1)} %broadcast_compare_fusion.2, f32[1,7,128,128]{3,2,1,0:T(8,128)S(1)} %get-tuple-element.237, f32[7,128]{1,0:T(8,128)S(1)} %get-tuple-element.220, ...), kind=kOutput, calls=%fused_computation.6.clone.1 | convolution fusion | flops 89456640 | bytes 2448897 | tf_op jit(solution)/shard_map/while/body/eval_jaxpr/hgqk,khd->hgqd/dot_general | solution.py:104
  81.8 0.3 fusion.45
  82.1 0.6 dynamic_slice.56
  84.7 0.1 broadcast_compare_fusion.2
  84.8 1.3 %select_reduce_fusion.2 = (f32[7,128]{1,0:T(8,128)S(1)}, f32[1,7,128,384]{2,3,1,0:T(8,128)S(1)}) fusion(pred[128,384]{0,1:T(8,128)(4,1)S(1)} %broadcast_compare_fusion.2, bf16[128,1,7,128]{3,0,2,1:T(8,128)(2,1)S(1)} %get-tuple-element.255, bf16[8,384,128]{2,1,0:T(8,128)(2,1)} %get-tuple-element.254, s32[]{:T(128)} %get-tuple-element.234), kind=kOutput, calls=%fused_computation.4.clone.1 | convolution fusion | flops 89111680 | bytes 1757184 | tf_op jit(solution)/shard_map/while/body/eval_jaxpr/qhgd,khd->hgqk/dot_general | solution.py:91
  86.1 1.4 %fusion.46 = f32[1,7,128,128]{3,2,1,0:T(8,128)S(1)} fusion(f32[1,7,128,384]{2,3,1,0:T(8,128)S(1)} %get-tuple-element.219, f32[7,128]{1,0:T(8,128)S(1)} %bitcast.92, pred[128,384]{0,1:T(8,128)(4,1)S(1)} %broadcast_compare_fusion.2, f32[1,7,128,128]{3,2,1,0:T(8,128)S(1)} %get-tuple-element.237, f32[7,128]{1,0:T(8,128)S(1)} %get-tuple-element.220, ...), kind=kOutput, calls=%fused_computation.6.clone.1 | convolution fusion | flops 89456640 | bytes 2448897 | tf_op jit(solution)/shard_map/while/body/eval_jaxpr/hgqk,khd->hgqd/dot_general | solution.py:104
  87.6 0.3 fusion.45
  87.9 0.6 dynamic_slice.56
  90.5 0.1 broadcast_compare_fusion.2
  90.6 1.3 %select_reduce_fusion.2 = (f32[7,128]{1,0:T(8,128)S(1)}, f32[1,7,128,384]{2,3,1,0:T(8,128)S(1)}) fusion(pred[128,384]{0,1:T(8,128)(4,1)S(1)} %broadcast_compare_fusion.2, bf16[128,1,7,128]{3,0,2,1:T(8,128)(2,1)S(1)} %get-tuple-element.255, bf16[8,384,128]{2,1,0:T(8,128)(2,1)} %get-tuple-element.254, s32[]{:T(128)} %get-tuple-element.234), kind=kOutput, calls=%fused_computation.4.clone.1 | convolution fusion | flops 89111680 | bytes 1757184 | tf_op jit(solution)/shard_map/while/body/eval_jaxpr/qhgd,khd->hgqk/dot_general | solution.py:91
  91.9 1.4 %fusion.46 = f32[1,7,128,128]{3,2,1,0:T(8,128)S(1)} fusion(f32[1,7,128,384]{2,3,1,0:T(8,128)S(1)} %get-tuple-element.219, f32[7,128]{1,0:T(8,128)S(1)} %bitcast.92, pred[128,384]{0,1:T(8,128)(4,1)S(1)} %broadcast_compare_fusion.2, f32[1,7,128,128]{3,2,1,0:T(8,128)S(1)} %get-tuple-element.237, f32[7,128]{1,0:T(8,128)S(1)} %get-tuple-element.220, ...), kind=kOutput, calls=%fused_computation.6.clone.1 | convolution fusion | flops 89456640 | bytes 2448897 | tf_op jit(solution)/shard_map/while/body/eval_jaxpr/hgqk,khd->hgqd/dot_general | solution.py:104
  93.3 0.3 fusion.45
  93.6 0.6 dynamic_slice.56
  96.3 0.1 broadcast_compare_fusion.2
  96.4 1.3 %select_reduce_fusion.2 = (f32[7,128]{1,0:T(8,128)S(1)}, f32[1,7,128,384]{2,3,1,0:T(8,128)S(1)}) fusion(pred[128,384]{0,1:T(8,128)(4,1)S(1)} %broadcast_compare_fusion.2, bf16[128,1,7,128]{3,0,2,1:T(8,128)(2,1)S(1)} %get-tuple-element.255, bf16[8,384,128]{2,1,0:T(8,128)(2,1)} %get-tuple-element.254, s32[]{:T(128)} %get-tuple-element.234), kind=kOutput, calls=%fused_computation.4.clone.1 | convolution fusion | flops 89111680 | bytes 1757184 | tf_op jit(solution)/shard_map/while/body/eval_jaxpr/qhgd,khd->hgqk/dot_general | solution.py:91
  97.7 1.4 %fusion.46 = f32[1,7,128,128]{3,2,1,0:T(8,128)S(1)} fusion(f32[1,7,128,384]{2,3,1,0:T(8,128)S(1)} %get-tuple-element.219, f32[7,128]{1,0:T(8,128)S(1)} %bitcast.92, pred[128,384]{0,1:T(8,128)(4,1)S(1)} %broadcast_compare_fusion.2, f32[1,7,128,128]{3,2,1,0:T(8,128)S(1)} %get-tuple-element.237, f32[7,128]{1,0:T(8,128)S(1)} %get-tuple-element.220, ...), kind=kOutput, calls=%fused_computation.6.clone.1 | convolution fusion | flops 89456640 | bytes 2448897 | tf_op jit(solution)/shard_map/while/body/eval_jaxpr/hgqk,khd->hgqd/dot_general | solution.py:104
  99.1 0.3 fusion.45
  99.4 0.6 dynamic_slice.56
  102.0 0.1 broadcast_compare_fusion.2
  102.2 1.3 %select_reduce_fusion.2 = (f32[7,128]{1,0:T(8,128)S(1)}, f32[1,7,128,384]{2,3,1,0:T(8,128)S(1)}) fusion(pred[128,384]{0,1:T(8,128)(4,1)S(1)} %broadcast_compare_fusion.2, bf16[128,1,7,128]{3,0,2,1:T(8,128)(2,1)S(1)} %get-tuple-element.255, bf16[8,384,128]{2,1,0:T(8,128)(2,1)} %get-tuple-element.254, s32[]{:T(128)} %get-tuple-element.234), kind=kOutput, calls=%fused_computation.4.clone.1 | convolution fusion | flops 89111680 | bytes 1757184 | tf_op jit(solution)/shard_map/while/body/eval_jaxpr/qhgd,khd->hgqk/dot_general | solution.py:91
  103.5 1.4 %fusion.46 = f32[1,7,128,128]{3,2,1,0:T(8,128)S(1)} fusion(f32[1,7,128,384]{2,3,1,0:T(8,128)S(1)} %get-tuple-element.219, f32[7,128]{1,0:T(8,128)S(1)} %bitcast.92, pred[128,384]{0,1:T(8,128)(4,1)S(1)} %broadcast_compare_fusion.2, f32[1,7,128,128]{3,2,1,0:T(8,128)S(1)} %get-tuple-element.237, f32[7,128]{1,0:T(8,128)S(1)} %get-tuple-element.220, ...), kind=kOutput, calls=%fused_computation.6.clone.1 | convolution fusion | flops 89456640 | bytes 2448897 | tf_op jit(solution)/shard_map/while/body/eval_jaxpr/hgqk,khd->hgqd/dot_general | solution.py:104
  104.9 0.3 fusion.45
  105.2 0.6 dynamic_slice.56
  107.8 0.1 broadcast_compare_fusion.2
  107.9 1.3 %select_reduce_fusion.2 = (f32[7,128]{1,0:T(8,128)S(1)}, f32[1,7,128,384]{2,3,1,0:T(8,128)S(1)}) fusion(pred[128,384]{0,1:T(8,128)(4,1)S(1)} %broadcast_compare_fusion.2, bf16[128,1,7,128]{3,0,2,1:T(8,128)(2,1)S(1)} %get-tuple-element.255, bf16[8,384,128]{2,1,0:T(8,128)(2,1)} %get-tuple-element.254, s32[]{:T(128)} %get-tuple-element.234), kind=kOutput, calls=%fused_computation.4.clone.1 | convolution fusion | flops 89111680 | bytes 1757184 | tf_op jit(solution)/shard_map/while/body/eval_jaxpr/qhgd,khd->hgqk/dot_general | solution.py:91
  109.2 1.4 %fusion.46 = f32[1,7,128,128]{3,2,1,0:T(8,128)S(1)} fusion(f32[1,7,128,384]{2,3,1,0:T(8,128)S(1)} %get-tuple-element.219, f32[7,128]{1,0:T(8,128)S(1)} %bitcast.92, pred[128,384]{0,1:T(8,128)(4,1)S(1)} %broadcast_compare_fusion.2, f32[1,7,128,128]{3,2,1,0:T(8,128)S(1)} %get-tuple-element.237, f32[7,128]{1,0:T(8,128)S(1)} %get-tuple-element.220, ...), kind=kOutput, calls=%fused_computation.6.clone.1 | convolution fusion | flops 89456640 | bytes 2448897 | tf_op jit(solution)/shard_map/while/body/eval_jaxpr/hgqk,khd->hgqd/dot_general | solution.py:104
  110.7 0.3 fusion.45
  111.0 0.6 dynamic_slice.56
  113.6 0.1 broadcast_compare_fusion.2
  113.7 1.3 %select_reduce_fusion.2 = (f32[7,128]{1,0:T(8,128)S(1)}, f32[1,7,128,384]{2,3,1,0:T(8,128)S(1)}) fusion(pred[128,384]{0,1:T(8,128)(4,1)S(1)} %broadcast_compare_fusion.2, bf16[128,1,7,128]{3,0,2,1:T(8,128)(2,1)S(1)} %get-tuple-element.255, bf16[8,384,128]{2,1,0:T(8,128)(2,1)} %get-tuple-element.254, s32[]{:T(128)} %get-tuple-element.234), kind=kOutput, calls=%fused_computation.4.clone.1 | convolution fusion | flops 89111680 | bytes 1757184 | tf_op jit(solution)/shard_map/while/body/eval_jaxpr/qhgd,khd->hgqk/dot_general | solution.py:91
  115.0 1.4 %fusion.46 = f32[1,7,128,128]{3,2,1,0:T(8,128)S(1)} fusion(f32[1,7,128,384]{2,3,1,0:T(8,128)S(1)} %get-tuple-element.219, f32[7,128]{1,0:T(8,128)S(1)} %bitcast.92, pred[128,384]{0,1:T(8,128)(4,1)S(1)} %broadcast_compare_fusion.2, f32[1,7,128,128]{3,2,1,0:T(8,128)S(1)} %get-tuple-element.237, f32[7,128]{1,0:T(8,128)S(1)} %get-tuple-element.220, ...), kind=kOutput, calls=%fused_computation.6.clone.1 | convolution fusion | flops 89456640 | bytes 2448897 | tf_op jit(solution)/shard_map/while/body/eval_jaxpr/hgqk,khd->hgqd/dot_general | solution.py:104
  116.5 0.3 fusion.45
  116.7 0.2 copy.26
  117.0 0.8 copy.27
  (70 shorter events, 1.2 us)
Async XLA Ops:
  6.5 11.5 %copy-start = (bf16[3584,128]{1,0:T(8,128)(2,1)S(1)}, bf16[3584,128]{1,0:T(8,128)(2,1)}, u32[]{:S(2)}) copy-start(bf16[3584,128]{1,0:T(8,128)(2,1)} %param.18) | copy-start | bytes 2752516
  6.5 11.5 %copy-start.4 = (f32[3584]{0:T(1024)S(1)}, f32[3584]{0:T(1024)}, u32[]{:S(2)}) copy-start(f32[3584]{0:T(1024)} %param.15) | copy-start | bytes 43012
  6.5 11.5 %copy-start.6 = (f32[128]{0:T(128)S(1)}, f32[128]{0:T(128)}, u32[]{:S(2)}) copy-start(f32[128]{0:T(128)} %param.19) | copy-start | bytes 1540
  6.5 61.4 %all-gather.2.cloned.1.call-start = ((), (), s32[]{:S(2)}) async-start(), calls=%async_computation | async-start | bytes 1769472 | tf_op jit(solution)/shard_map/all_gather | solution.py:42
  17.8 2.6 %copy-start.7 = (f32[128]{0:T(128)S(1)}, f32[128]{0:T(128)}, u32[]{:S(2)}) copy-start(f32[128]{0:T(128)} %param.21) | copy-start | bytes 1540
  18.7 3.4 %copy-start.1 = (bf16[256,128]{1,0:T(8,128)(2,1)S(1)}, bf16[256,128]{1,0:T(8,128)(2,1)}, u32[]{:S(2)}) copy-start(bf16[256,128]{1,0:T(8,128)(2,1)} %param.23) | copy-start | bytes 196612
  18.7 3.4 %copy-start.2 = (bf16[256,128]{1,0:T(8,128)(2,1)S(1)}, bf16[256,128]{1,0:T(8,128)(2,1)}, u32[]{:S(2)}) copy-start(bf16[256,128]{1,0:T(8,128)(2,1)} %param.22) | copy-start | bytes 196612
  20.0 2.8 %copy-start.5 = (f32[896]{0:T(1024)S(1)}, f32[896]{0:T(1024)}, u32[]{:S(2)}) copy-start(f32[896]{0:T(1024)} %param.17) | copy-start | bytes 10756
  27.3 0.7 copy-start.3
Sparse Core Ops, SparseCore 0:
  22.9 44.9 all-gather.1
